TPU v7x, 32 devices: a whole 2x2x4 slice. The times are simulated.
32 devices in a mesh: dp: 8 (over y, x, core), fsdp: 4 (over z).
Axes of the slice: x: 2, y: 2, z: 4, core: 2. Of those that a mesh axis runs over, the one named last changes fastest.
Arguments:
- gradients: bfloat16 [8, 512, 8192], P('dp', None, 'fsdp'), may hold values from -1.5 to 1.5
- momentum: float32 [512, 8192], P('dp', 'fsdp'), may hold values from -1500 to 1500
- weight: float32 [512, 8192], P(None, 'fsdp'), may hold values from -3 to 3
- logit_peaks: int32 [32, 32], P(('dp', 'fsdp')), may hold values from 0 to 479, as said below
- clip_threshold: int32 [1], replicated, may hold values from 60 to 120
Outputs:
- new_weight: float32 [512, 8192], P(None, 'fsdp')
- new_momentum: float32 [512, 8192], P('dp', 'fsdp')
- update_norm: float32 [1], replicated
Inputs may be any that keep to these rules, and one draw needn't show every extreme that they name: `logit_peaks`: for every head, the largest entry over all rows is at least 40.
All inputs are finite; a program needn't handle non-finite values.
Results may differ from a plain program's by a relative error of at most 0.0023.
Values may be sent and summed in bfloat16 or wider, within the bound.
A program may use at most 64 MiB of HBM per device.

v0:
```python
import math

import jax
import jax.numpy as jnp
from jax import lax
from jax.sharding import PartitionSpec as P

KVL = 512
NOPE = 128
VDIM = 128
HEADS = 32
ITERS = 3
KVO = 8192


quintic_terms = (3.4445, -4.775, 2.0315)
learning_rate = 0.5
weight_decay = 0.1
momentum_decay = 0.95
update_gain = 0.2
epsilon = 1e-07


def column_factors(global_peaks, clip_threshold):
    largest = jnp.max(global_peaks, axis=0).astype(jnp.float32)
    clip_ratio = jnp.minimum(1.0, clip_threshold.astype(jnp.float32)[0] / largest)
    key_scale = jnp.sqrt(clip_ratio)
    per_head = jnp.concatenate(
        [jnp.broadcast_to(key_scale[:, None], (HEADS, NOPE)), jnp.ones((HEADS, VDIM), jnp.float32)],
        axis=1,
    )
    return per_head.reshape(HEADS * (NOPE + VDIM))


def gram_over_replicas(partial_gram):
    return lax.psum(partial_gram.astype(jnp.bfloat16), "dp").astype(jnp.float32)


def newton_schulz(column_block, gram_sum):
    current = column_block
    for iteration in range(ITERS):
        partial_gram = lax.dot_general(
            current,
            current,
            (((1,), (1,)), ((), ())),
            precision=lax.Precision.HIGHEST,
            preferred_element_type=jnp.float32,
        )
        square = gram_sum(partial_gram)
        combined = quintic_terms[1] * square + quintic_terms[2] * jnp.dot(
            square, square, precision=lax.Precision.HIGHEST, preferred_element_type=jnp.float32
        )
        current = quintic_terms[0] * current + jnp.dot(
            combined, current, precision=lax.Precision.HIGHEST, preferred_element_type=jnp.float32
        )
    return current


def local(gradients, momentum, weight, logit_peaks, clip_threshold):
    replica_shard = gradients[0].astype(jnp.float32)
    summed = lax.psum_scatter(
        replica_shard.astype(jnp.bfloat16), "dp", scatter_dimension=0, tiled=True
    ).astype(jnp.float32)
    new_momentum = momentum_decay * momentum + summed
    blended = summed + momentum_decay * new_momentum
    global_peaks = lax.pmax(logit_peaks, ("dp", "fsdp"))
    square_total = lax.psum(jnp.sum(blended * blended), ("dp", "fsdp"))
    update_norm = jnp.sqrt(square_total / (KVL * KVO)).reshape(1)
    normalized = blended / (jnp.sqrt(square_total) + epsilon)
    dp_count = lax.axis_size("dp")
    fsdp_count = lax.axis_size("fsdp")
    row_count = normalized.shape[0]
    shard_cols = normalized.shape[1]
    piece_cols = shard_cols // dp_count
    wide_rows = lax.all_gather(normalized.astype(jnp.bfloat16), "fsdp", axis=1, tiled=True).astype(
        normalized.dtype
    )
    split_up = wide_rows.reshape(row_count, fsdp_count, dp_count, piece_cols)
    columns = lax.all_to_all(
        split_up.astype(jnp.bfloat16), "dp", split_axis=2, concat_axis=0, tiled=True
    ).astype(split_up.dtype)
    column_block = columns.reshape(KVL, fsdp_count * piece_cols)
    orthogonal = newton_schulz(column_block, gram_over_replicas)
    orthogonal_all = orthogonal.reshape(KVL, fsdp_count, piece_cols)
    own_block = lax.dynamic_index_in_dim(orthogonal_all, lax.axis_index("fsdp"), 1, keepdims=False)
    shard_orthogonal = lax.all_gather(
        own_block.astype(jnp.bfloat16), "dp", axis=1, tiled=True
    ).astype(own_block.dtype)
    update_scale = update_gain * math.sqrt(max(KVL, KVO))
    stepped = weight - learning_rate * (update_scale * shard_orthogonal + weight_decay * weight)
    factors = column_factors(global_peaks, clip_threshold)
    shard_factors = lax.dynamic_slice_in_dim(
        factors, lax.axis_index("fsdp") * shard_cols, shard_cols
    )
    new_weight = stepped * shard_factors[None, :]
    return (new_weight, new_momentum, update_norm)


def solution(mesh):
    placed = (P("dp", None, "fsdp"), P("dp", "fsdp"), P(None, "fsdp"), P(("dp", "fsdp"), None), P())
    return jax.shard_map(
        local,
        mesh=mesh,
        in_specs=placed,
        out_specs=(P(None, "fsdp"), P("dp", "fsdp"), P()),
        check_vma=False,
    )
```

profile of v0, /device:TPU:0, one launch (start us, length us, event | category | flops | bytes accessed | tf_op | source)
XLA Modules:
  0.0 393.2 jit_solution(4246581110344312407)
XLA Ops:
  8.0 47.2 %reduce-scatter.2.cloned.1.call-done = bf16[64,2048]{1,0:T(8,128)(2,1)} async-done(((bf16[512,2048]{1,0:T(8,128)(2,1)}), bf16[64,2048]{1,0:T(8,128)(2,1)}) %reduce-scatter.2.cloned.1.call-update) | async-done | bytes 262160 | tf_op jit(solution)/shard_map/reduce_scatter | solution.py:61
  55.1 1.7 multiply_reduce_fusion
  56.8 39.5 %psum.28 = f32[]{:T(128)} all-reduce(f32[]{:T(128)} %get-tuple-element.3), channel_id=1, replica_groups=mesh['dp'=8,'fsdp'=4] {'dp','fsdp'}, use_global_device_ids=true, to_apply=%region_2.0 | all-reduce | flops 1 | bytes 8 | tf_op jit(solution)/shard_map/psum | solution.py:67
  97.0 1.7 divide_convert_fusion
  98.8 29.1 %all-gather.4.cloned.1.call-done = bf16[64,8192]{1,0:T(8,128)(2,1)} async-done(((bf16[64,2048]{1,0:T(8,128)(2,1)}), bf16[64,8192]{1,0:T(8,128)(2,1)}) %all-gather.4.cloned.1.call-update) | async-done | bytes 1048592 | tf_op jit(solution)/shard_map/all_gather | solution.py:75
  127.9 1.5 copy.11
  129.8 18.8 %all_to_all.18 = bf16[64,4,8,256]{3,1,0,2:T(4,128)(2,1)S(1)} all-to-all(bf16[64,4,8,256]{3,1,0,2:T(4,128)(2,1)S(1)} %copy.8), channel_id=1, replica_groups=mesh['dp'=8,'fsdp'=4] {'dp'}, dimensions={2} | all-to-all | bytes 2097152 | tf_op jit(solution)/shard_map/all_to_all | solution.py:79
  148.8 1.5 convolution_convert_fusion.2
  150.4 52.5 %all-reduce.5.cloned.1.call-done = bf16[512,512]{1,0:T(8,128)(2,1)} async-done(((bf16[512,512]{1,0:T(8,128)(2,1)}), bf16[512,512]{1,0:T(8,128)(2,1)}) %all-reduce.5.cloned.1.call-update) | async-done | bytes 524304 | tf_op jit(solution)/shard_map/psum | solution.py:36
  202.9 1.9 fusion.5
  204.8 1.8 multiply_add_fusion.2
  206.6 1.3 copy-done
  207.9 4.3 %convolution_convert_fusion.1 = bf16[512,512]{1,0:T(8,128)(2,1)} fusion(f32[512,1024]{1,0:T(8,128)S(1)} %multiply_add_fusion.2), kind=kOutput, calls=%fused_computation.14 | convolution fusion | flops 3221487616 | bytes 2621440 | tf_op jit(solution)/shard_map/dot_general | solution.py:42
  212.5 54.0 %all-reduce.7.cloned.1.call-done = bf16[512,512]{1,0:T(8,128)(2,1)} async-done(((bf16[512,512]{1,0:T(8,128)(2,1)}), bf16[512,512]{1,0:T(8,128)(2,1)}) %all-reduce.7.cloned.1.call-update) | async-done | bytes 524304 | tf_op jit(solution)/shard_map/psum | solution.py:36
  266.5 1.9 fusion.4
  268.6 3.7 multiply_add_fusion.1
  272.2 4.3 %convolution_convert_fusion = bf16[512,512]{1,0:T(8,128)(2,1)} fusion(f32[512,1024]{1,0:T(8,128)S(1)} %multiply_add_fusion.1), kind=kOutput, calls=%fused_computation.13 | convolution fusion | flops 3221487616 | bytes 2621440 | tf_op jit(solution)/shard_map/dot_general | solution.py:42
  276.6 54.2 %all-reduce.9.cloned.1.call-done = bf16[512,512]{1,0:T(8,128)(2,1)} async-done(((bf16[512,512]{1,0:T(8,128)(2,1)}), bf16[512,512]{1,0:T(8,128)(2,1)}) %all-reduce.9.cloned.1.call-update) | async-done | bytes 524304 | tf_op jit(solution)/shard_map/psum | solution.py:36
  330.9 1.9 fusion.3
  332.8 3.6 multiply_add_fusion
  336.4 0.8 reshape.40
  337.7 0.7 copy.15
  338.5 39.3 %pmax.7 = s32[1,32]{1,0:T(1,128)S(1)} all-reduce(s32[1,32]{1,0:T(1,128)S(1)} %copy-done.4), channel_id=1, replica_groups=mesh['dp'=8,'fsdp'=4] {'dp','fsdp'}, use_global_device_ids=true, to_apply=%region_6.0 | all-reduce | flops 32 | bytes 256 | tf_op jit(solution)/shard_map/pmax | solution.py:66
  379.3 5.9 %fusion.2 = f32[512,2048]{1,0:T(8,128)} fusion(f32[512,2048]{1,0:T(8,128)} %param.7, bf16[512,1,2048]{2,0,1:T(8,128)(2,1)} %all-gather.6.cloned.1.call-done, f32[2048]{0:T(1024)S(1)} %dynamic_slice.8), kind=kLoop, calls=%fused_computation.3 | loop fusion | flops 7340032 | bytes 10493952 | tf_op jit(solution)/shard_map/mul | solution.py:95
  (30 shorter events, 2.6 us)
Async XLA Ops:
  7.2 48.0 %copy-start.3 = (f32[64,2048]{1,0:T(8,128)S(1)}, f32[64,2048]{1,0:T(8,128)}, u32[]{:S(2)}) copy-start(f32[64,2048]{1,0:T(8,128)} %param.6) | copy-start | bytes 1572868
  7.2 48.0 %reduce-scatter.2.cloned.1.call-start = ((), (), s32[]{:S(2)}) async-start(), calls=%async_computation.2 | async-start | bytes 2359296 | tf_op jit(solution)/shard_map/reduce_scatter | solution.py:61
  7.9 120.0 %all-gather.4.cloned.1.call-start = ((), (), s32[]{:S(2)}) async-start(), calls=%async_computation.3 | async-start | bytes 1310720 | tf_op jit(solution)/shard_map/all_gather | solution.py:75
  56.8 72.9 %copy-start.2 = (f32[64,2048]{1,0:T(8,128)}, f32[64,2048]{1,0:T(8,128)S(1)}, u32[]{:S(2)}) copy-start(f32[64,2048]{1,0:T(8,128)S(1)} %get-tuple-element.4) | copy-start | bytes 1572868
  98.7 104.1 %all-reduce.5.cloned.1.call-start = ((), (), s32[]{:S(2)}) async-start(), calls=%async_computation.4 | async-start | bytes 1048576 | tf_op jit(solution)/shard_map/psum | solution.py:36
  150.3 116.2 %all-reduce.7.cloned.1.call-start = ((), (), s32[]{:S(2)}) async-start(), calls=%async_computation.5 | async-start | bytes 1048576 | tf_op jit(solution)/shard_map/psum | solution.py:36
  206.6 1.3 copy-start
  212.3 118.6 %all-reduce.9.cloned.1.call-start = ((), (), s32[]{:S(2)}) async-start(), calls=%async_computation.6 | async-start | bytes 1048576 | tf_op jit(solution)/shard_map/psum | solution.py:36
  266.5 2.1 copy-start.1
  276.6 102.7 %all-gather.6.cloned.1.call-start = ((), (), s32[]{:S(2)}) async-start(), calls=%async_computation.7 | async-start | bytes 2359296 | tf_op jit(solution)/shard_map/all_gather | solution.py:86
  336.4 2.1 copy-start.4
Sparse Core Ops, SparseCore 0:
  11.3 43.8 reduce-scatter.1
  98.9 28.9 all-gather.3
  150.5 52.3 all-reduce.4
  212.4 54.0 all-reduce.6
  276.7 54.1 all-reduce.8
  338.6 27.4 all-gather.5
where the time goes:
time: 394 us; the launch traced here: 393 us
  waiting for transfers between devices  238 us (60%)
  blocking collectives  97.5 us (25%)
  matrix products  25 us (6%)
  between operations  17.4 us (4%)
  other arithmetic  9.38 us (2%)
  local copies, waits for them, and re-layouts  5.74 us (1%)
    psum x3, waiting for transfers between devices, gram_over_replicas(): return lax.psum(partial_gram.astype(jnp.bfloat16), 'dp').astype(jnp.float32)  161 us
    reduce_scatter x1, waiting for transfers between devices, local(): lax.psum_scatter(replica_shard.astype(jnp.bfloat16), 'dp', scatter_dimens...  47.2 us
    psum x1, blocking collectives, local(): square_total = lax.psum(jnp.sum(blended * blended), ('dp', 'fsdp'))  39.5 us
    pmax x1, blocking collectives, local(): global_peaks = lax.pmax(logit_peaks, ('dp', 'fsdp'))  39.3 us
    all_gather x1, waiting for transfers between devices, local(): lax.all_gather(normalized.astype(jnp.bfloat16), 'fsdp', axis=1, tiled=True)  29.1 us
    all_to_all x1, blocking collectives, local(): lax.all_to_all(split_up.astype(jnp.bfloat16), 'dp', split_axis=2, concat_...  18.8 us
    dot_general x3, matrix products, newton_schulz(): lax.dot_general(current, current, (((1,), (1,)), ((), ())), precision=lax...  10.2 us
    dot_general x3, matrix products, newton_schulz(): jnp.dot(combined, current, precision=lax.Precision.HIGHEST, preferred_ele...  9.1 us
  transfers between devices with their start and end apart: 6, of which 5 were waited for; matrix products, arithmetic and copies ran while one was open for 0% of the time, Pallas kernels for 0%

commit v1 on v0

v1 whole, which is shorter than its diff:
```python
import functools
import math

import jax
import jax.numpy as jnp
from jax import lax
from jax.experimental import pallas as pl
from jax.experimental.pallas import tpu as pltpu
from jax.sharding import PartitionSpec as P

KVL = 512
NOPE = 128
VDIM = 128
HEADS = 32
ITERS = 3
KVO = 8192


quintic_terms = (3.4445, -4.775, 2.0315)
learning_rate = 0.5
weight_decay = 0.1
momentum_decay = 0.95
update_gain = 0.2
epsilon = 1e-07


def head_factors(largest, clip_threshold):
    clip_ratio = jnp.minimum(1.0, clip_threshold.astype(jnp.float32)[0] / largest)
    key_scale = jnp.sqrt(clip_ratio)
    per_head = jnp.concatenate(
        [jnp.broadcast_to(key_scale[:, None], (HEADS, NOPE)), jnp.ones((HEADS, VDIM), jnp.float32)],
        axis=1,
    )
    return per_head.reshape(HEADS * (NOPE + VDIM))


def product(left, right):
    return jnp.dot(left, right, precision=lax.Precision.HIGH, preferred_element_type=jnp.float32)


def polynomial_of_gram(gram):
    lead, second, third = quintic_terms
    whole = None
    for iteration in range(ITERS):
        rest = second * gram + third * product(gram, gram)
        if whole is None:
            whole = lead * jnp.eye(KVL, dtype=jnp.float32) + rest
        else:
            whole = lead * whole + product(rest, whole)
        if iteration < ITERS - 1:
            half = lead * gram + product(rest, gram)
            gram = lead * half + product(half, rest)
    return whole


CHUNKS = 2
MESH = pl.DeviceIdType.MESH


def exchange(
    dp_count,
    fsdp_count,
    grad,
    momentum,
    peaks,
    new_momentum,
    columns,
    gram,
    stats_out,
    pair,
    outgoing,
    incoming,
    gram_own,
    gram_in,
    stats,
    stats_in,
    stats_wide,
    stats_wide_in,
    pair_send,
    pair_recv,
    rs_send,
    rs_recv,
    ag_send,
    ag_recv,
    fw_send,
    fw_recv,
    gz_send,
    gz_recv,
    st_send,
    st_recv,
    sz_send,
    sz_recv,
    gg_send,
    gg_recv,
    gf_send,
    gf_recv,
):
    d = lax.axis_index("dp")
    f = lax.axis_index("fsdp")
    chips = dp_count // 2
    q = d // 2
    core = d % 2
    rows = momentum.shape[0]
    width = momentum.shape[1] // CHUNKS
    partner = 2 * q + 1 - core

    barrier = pltpu.get_barrier_semaphore()
    for k in range(1, dp_count):
        pl.semaphore_signal(
            barrier, inc=1, device_id=(lax.rem(d + k, dp_count), f), device_id_type=MESH
        )
    for k in range(1, fsdp_count):
        pl.semaphore_signal(
            barrier, inc=1, device_id=(d, lax.rem(f + k, fsdp_count)), device_id_type=MESH
        )
    pl.semaphore_wait(barrier, dp_count + fsdp_count - 2)

    def send(source, target, send_sem, recv_sem, device):
        copy = pltpu.make_async_remote_copy(
            src_ref=source,
            dst_ref=target,
            send_sem=send_sem,
            recv_sem=recv_sem,
            device_id=device,
            device_id_type=MESH,
        )
        copy.start()
        return copy

    def block(device):
        return pl.ds(pl.multiple_of(device * rows, rows), rows)

    def chunk(h):
        return pl.ds(h * width, width)

    def ahead(k):
        return lax.rem(q + k, chips)

    def behind(k):
        return lax.rem(q + chips - k, chips)

    offsets = list(range(1, chips)) + [0]
    paired = {}
    for h in range(CHUNKS):
        for k in offsets:
            paired[h, k] = send(
                grad.at[block(2 * ahead(k) + 1 - core), chunk(h)],
                pair.at[h, k],
                pair_send.at[h, k],
                pair_recv.at[h, k],
                (partner, f),
            )
    scattered = {}
    for h in range(CHUNKS):
        for k in range(1, chips):
            paired[h, k].wait_recv()
            here = grad[block(2 * ahead(k) + core), chunk(h)].astype(jnp.float32)
            outgoing[h, k] = (here + pair[h, k].astype(jnp.float32)).astype(jnp.bfloat16)
            scattered[h, k] = send(
                outgoing.at[h, k],
                incoming.at[h, k],
                rs_send.at[h, k],
                rs_recv.at[h, k],
                (2 * ahead(k) + core, f),
            )
    gathered = {}
    forwarded = {}
    square_sum = jnp.float32(0.0)
    for h in range(CHUNKS):
        paired[h, 0].wait_recv()
        summed = grad[block(d), chunk(h)].astype(jnp.float32) + pair[h, 0].astype(jnp.float32)
        for k in range(1, chips):
            scattered[h, k].wait_recv()
            summed = summed + incoming[h, k].astype(jnp.float32)
        updated = momentum_decay * momentum[:, chunk(h)] + summed
        new_momentum[:, chunk(h)] = updated
        blended = summed + momentum_decay * updated
        columns[block(d), chunk(h)] = blended.astype(jnp.bfloat16)
        mine = columns.at[block(d), chunk(h)]
        for k in range(1, chips):
            gathered[h, k] = send(
                mine, mine, ag_send.at[h, k], ag_recv.at[h, k], (2 * ahead(k) + core, f)
            )
        forwarded[h, 0] = send(mine, mine, fw_send.at[h, 0], fw_recv.at[h, 0], (partner, f))
        square_sum = square_sum + jnp.sum(blended * blended)

    stats[0:8] = peaks[...]
    stats[8:16] = jnp.full((8, 128), square_sum, jnp.float32)
    stat_copies = [
        send(
            stats,
            stats_in.at[k],
            st_send.at[k],
            st_recv.at[k],
            (lax.rem(d + k, dp_count), f),
        )
        for k in range(1, dp_count)
    ]

    own_gram = jnp.zeros((rows, gram.shape[0]), jnp.float32)
    for h in range(CHUNKS):
        for k in range(1, chips):
            gathered[h, k].wait_recv()
            there = columns.at[block(2 * behind(k) + core), chunk(h)]
            forwarded[h, k] = send(
                there, there, fw_send.at[h, k], fw_recv.at[h, k], (partner, f)
            )
    for copy in stat_copies:
        copy.wait_recv()
    top = stats[0:8]
    level = stats[8:16]
    for k in range(1, dp_count):
        top = jnp.maximum(top, stats_in[k, 0:8])
        level = level + stats_in[k, 8:16]
    stats_wide[0:8] = top
    stats_wide[8:16] = level
    wide_copies = [
        send(
            stats_wide,
            stats_wide_in.at[k],
            sz_send.at[k],
            sz_recv.at[k],
            (d, lax.rem(f + k, fsdp_count)),
        )
        for k in range(1, fsdp_count)
    ]
    for h in range(CHUNKS):
        for k in range(chips):
            forwarded[h, k].wait_recv()
        own_gram = own_gram + lax.dot_general(
            columns[block(d), chunk(h)],
            columns[:, chunk(h)],
            (((1,), (1,)), ((), ())),
            preferred_element_type=jnp.float32,
        )

    gram_own[...] = own_gram.astype(jnp.bfloat16)
    gram_copies = [
        send(
            gram_own,
            gram_in.at[k],
            gz_send.at[k],
            gz_recv.at[k],
            (d, lax.rem(f + k, fsdp_count)),
        )
        for k in range(1, fsdp_count)
    ]
    for copy in wide_copies:
        copy.wait_recv()
    for k in range(1, fsdp_count):
        top = jnp.maximum(top, stats_wide_in[k, 0:8])
        level = level + stats_wide_in[k, 8:16]
    stats_out[0:8] = top
    stats_out[8:16] = level
    for copy in gram_copies:
        copy.wait_recv()
    for k in range(1, fsdp_count):
        own_gram = own_gram + gram_in[k].astype(jnp.float32)
    gram[block(d)] = own_gram.astype(jnp.bfloat16)
    mine = gram.at[block(d)]
    gram_gathered = {}
    gram_forwarded = {}
    for k in range(1, chips):
        gram_gathered[k] = send(
            mine, mine, gg_send.at[k], gg_recv.at[k], (2 * ahead(k) + core, f)
        )
    gram_forwarded[0] = send(mine, mine, gf_send.at[0], gf_recv.at[0], (partner, f))
    for k in range(1, chips):
        gram_gathered[k].wait_recv()
        there = gram.at[block(2 * behind(k) + core)]
        gram_forwarded[k] = send(there, there, gf_send.at[k], gf_recv.at[k], (partner, f))
    for k in range(chips):
        gram_forwarded[k].wait_recv()

    for group in (paired, scattered, gathered, forwarded, gram_gathered, gram_forwarded):
        for copy in group.values():
            copy.wait_send()
    for copy in stat_copies + wide_copies + gram_copies:
        copy.wait_send()


def reduce_and_gather(gradient, momentum, peaks):
    dp_count = lax.axis_size("dp")
    fsdp_count = lax.axis_size("fsdp")
    chips = dp_count // 2
    rows, shard_cols = momentum.shape
    width = shard_cols // CHUNKS
    in_vmem = pl.BlockSpec(memory_space=pltpu.VMEM)
    slots = pltpu.VMEM((CHUNKS, chips, rows, width), jnp.bfloat16)
    by_chunk = [pltpu.SemaphoreType.DMA((CHUNKS, chips))] * 8
    by_fsdp = [pltpu.SemaphoreType.DMA((fsdp_count,))] * 2
    by_dp = [pltpu.SemaphoreType.DMA((dp_count,))] * 2
    by_chip = [pltpu.SemaphoreType.DMA((chips,))] * 4
    return pl.pallas_call(
        functools.partial(exchange, dp_count, fsdp_count),
        out_shape=(
            jax.ShapeDtypeStruct((rows, shard_cols), jnp.float32),
            jax.ShapeDtypeStruct((KVL, shard_cols), jnp.bfloat16),
            jax.ShapeDtypeStruct((KVL, KVL), jnp.bfloat16),
            jax.ShapeDtypeStruct((16, 128), jnp.float32),
        ),
        in_specs=[in_vmem] * 3,
        out_specs=(in_vmem,) * 4,
        scratch_shapes=[
            slots,
            slots,
            slots,
            pltpu.VMEM((rows, KVL), jnp.bfloat16),
            pltpu.VMEM((fsdp_count, rows, KVL), jnp.bfloat16),
            pltpu.VMEM((16, 128), jnp.float32),
            pltpu.VMEM((dp_count, 16, 128), jnp.float32),
            pltpu.VMEM((16, 128), jnp.float32),
            pltpu.VMEM((fsdp_count, 16, 128), jnp.float32),
        ]
        + by_chunk
        + by_fsdp
        + by_dp
        + by_fsdp
        + by_chip,
        compiler_params=pltpu.CompilerParams(
            collective_id=0, has_side_effects=True, vmem_limit_bytes=40 * 1024 * 1024
        ),
    )(gradient, momentum, peaks)


def local(gradients, momentum, weight, logit_peaks, clip_threshold):
    peaks = jnp.zeros((8, 128), jnp.float32).at[:1, :HEADS].set(logit_peaks.astype(jnp.float32))
    new_momentum, columns, gram_total, stats = reduce_and_gather(gradients[0], momentum, peaks)
    largest = stats[0, :HEADS]
    square_total = stats[8, 0]
    update_norm = jnp.sqrt(square_total / (KVL * KVO)).reshape(1)
    inverse = 1.0 / (jnp.sqrt(square_total) + epsilon)
    gram = gram_total.astype(jnp.float32) * inverse * inverse
    whole = polynomial_of_gram(gram)
    orthogonal = inverse * jnp.dot(
        whole.astype(jnp.bfloat16), columns, preferred_element_type=jnp.float32
    )
    shard_cols = columns.shape[1]
    update_scale = update_gain * math.sqrt(max(KVL, KVO))
    stepped = weight - learning_rate * (update_scale * orthogonal + weight_decay * weight)
    factors = head_factors(largest, clip_threshold)
    shard_factors = lax.dynamic_slice_in_dim(
        factors, lax.axis_index("fsdp") * shard_cols, shard_cols
    )
    return (stepped * shard_factors[None, :], new_momentum, update_norm)


def solution(mesh):
    placed = (P("dp", None, "fsdp"), P("dp", "fsdp"), P(None, "fsdp"), P(("dp", "fsdp"), None), P())
    return jax.shard_map(
        local,
        mesh=mesh,
        in_specs=placed,
        out_specs=(P(None, "fsdp"), P("dp", "fsdp"), P()),
        check_vma=False,
    )
```

time: 394 us -> 68.9 us (0.17)
  waiting for transfers between devices: 238 us -> 0 us
  blocking collectives: 97.5 us -> 0 us
  Pallas kernels: 0 us -> 46.7 us
  between operations: 17.4 us -> 3.95 us
  matrix products: 25 us -> 13.3 us
  other arithmetic: 9.38 us -> 0.67 us
    psum x3 -> x0, waiting for transfers between devices: 161 us -> none  [gram_over_replicas(): return lax.psum(partial_gram.astype(jnp.bfloat16), 'dp').astype(jnp.float32)]
    reduce_scatter x1 -> x0, waiting for transfers between devices: 47.2 us -> none  [local(): lax.psum_scatter(replica_shard.astype(jnp.bfloat16), 'dp', scatter_dimens...]
    pallas_call x0 -> x1, Pallas kernels: none -> 46.7 us  [reduce_and_gather(): pl.pallas_call(functools.partial(exchange, dp_count, fsdp_count), out_sha...]
    psum x1 -> x0, blocking collectives: 39.5 us -> none  [local(): square_total = lax.psum(jnp.sum(blended * blended), ('dp', 'fsdp'))]
    pmax x1 -> x0, blocking collectives: 39.3 us -> none  [local(): global_peaks = lax.pmax(logit_peaks, ('dp', 'fsdp'))]
    all_gather x2 -> x0, waiting for transfers between devices: 29.1 us -> none  [the longest x1 29.1 us: local(): lax.all_gather(normalized.astype(jnp.bfloat16), 'fsdp', axis=1, tiled=True)]
    all_to_all x1 -> x0, blocking collectives: 18.8 us -> none  [local(): lax.all_to_all(split_up.astype(jnp.bfloat16), 'dp', split_axis=2, concat_...]
    dot_general x9 -> x10, matrix products: 25 us -> 13.3 us  [the longest x9 9.45 us: product(): jnp.dot(left, right, precision=lax.Precision.HIGH, preferred_element_type...]
  transfers between devices with their start and end apart: 6 -> 0, of which waited for: 5 -> 0; matrix products, arithmetic and copies ran while one was open for 0% -> 0% of each run, Pallas kernels for 0% -> 0%
where the time goes in v1:
time: 68.9 us; the launch traced here: 68.6 us
  Pallas kernels  46.7 us (68%)
  matrix products  13.3 us (19%)
  local copies, waits for them, and re-layouts  4.06 us (6%)
  between operations  3.95 us (6%)
    pallas_call x1, Pallas kernels, reduce_and_gather(): pl.pallas_call(functools.partial(exchange, dp_count, fsdp_count), out_sha...  46.7 us
    dot_general x9, matrix products, product(): jnp.dot(left, right, precision=lax.Precision.HIGH, preferred_element_type...  9.45 us
    dot_general x1, matrix products, local(): jnp.dot(whole.astype(jnp.bfloat16), columns, preferred_element_type=jnp.f...  3.85 us
    unnamed x9, local copies, waits for them, and re-layouts  3.46 us

profile of v1, /device:TPU:0, one launch (start us, length us, event | category | flops | bytes accessed | tf_op | source)
XLA Modules:
  0.0 68.6 jit_solution(9799394093713996385)
XLA Ops:
  1.3 0.7 convert_element_type.13
  1.9 0.0 copy-start
  1.9 1.6 %copy-done = bf16[1,512,2048]{2,1,0:T(8,128)(2,1)S(1)} copy-done((bf16[1,512,2048]{2,1,0:T(8,128)(2,1)S(1)}, bf16[1,512,2048]{2,1,0:T(8,128)(2,1)}, u32[]{:S(2)}) %copy-start) | copy-done | bytes 2097176
  3.5 0.0 copy-start.1
  3.5 1.0 %copy-done.1 = f32[64,2048]{1,0:T(8,128)S(1)} copy-done((f32[64,2048]{1,0:T(8,128)S(1)}, f32[64,2048]{1,0:T(8,128)}, u32[]{:S(2)}) %copy-start.1) | copy-done | bytes 524312
  4.6 46.7 %shard_map.76 = (f32[64,2048]{1,0:T(8,128)S(1)}, bf16[512,2048]{1,0:T(8,128)(2,1)S(1)}, bf16[512,512]{1,0:T(8,128)(2,1)S(1)}, f32[16,128]{1,0:T(8,128)S(1)}) custom-call(bf16[512,2048]{1,0:T(8,128)(2,1)S(1)} %bitcast.25, f32[64,2048]{1,0:T(8,128)S(1)} %copy-done.1, f32[8,128]{1,0:T(8,128)S(1)} %scatter.4.peaks), custom_call_target="tpu_custom_call" | custom-call | tf_op jit(solution)/shard_map/pallas_call | solution.py:294
  51.3 0.5 slice.26
  53.2 0.1 broadcast_in_dim.2
  53.3 1.1 %fusion.2 = f32[512,512]{1,0:T(8,128)S(1)} fusion(bf16[512,512]{1,0:T(8,128)(2,1)S(1)} %get-tuple-element.20, f32[]{:T(128)} %bitcast.1), kind=kOutput, calls=%fused_computation.12 | convolution fusion | flops 807665664 | bytes 1572868 | tf_op jit(solution)/shard_map/dot_general | solution.py:38
  54.5 1.1 %convolution_add_fusion.5 = f32[512,512]{1,0:T(8,128)S(1)} fusion(f32[512,512]{1,0:T(8,128)S(1)} %fusion.2, bf16[512,512]{1,0:T(8,128)(2,1)S(1)} %get-tuple-element.20, f32[]{:T(128)} %bitcast.1), kind=kOutput, calls=%fused_computation.10 | convolution fusion | flops 807403520 | bytes 2621444 | tf_op jit(solution)/shard_map/dot_general | solution.py:38
  55.6 1.0 %convolution_add_fusion.4 = f32[512,512]{1,0:T(8,128)S(1)} fusion(f32[512,512]{1,0:T(8,128)S(1)} %convolution_add_fusion.5, f32[512,512]{1,0:T(8,128)S(1)} %fusion.2), kind=kOutput, calls=%fused_computation.9 | convolution fusion | flops 805830656 | bytes 3145728 | tf_op jit(solution)/shard_map/dot_general | solution.py:38
  56.6 1.0 %fusion.1 = f32[512,512]{1,0:T(8,128)S(1)} fusion(f32[512,512]{1,0:T(8,128)S(1)} %convolution_add_fusion.4), kind=kOutput, calls=%fused_computation.8 | convolution fusion | flops 806092800 | bytes 2097152 | tf_op jit(solution)/shard_map/dot_general | solution.py:38
  57.6 1.0 %convolution_add_fusion.2 = f32[512,512]{1,0:T(8,128)S(1)} fusion(f32[512,512]{1,0:T(8,128)S(1)} %fusion.1, f32[512,512]{1,0:T(8,128)S(1)} %convolution_add_fusion.4), kind=kOutput, calls=%fused_computation.5 | convolution fusion | flops 805830656 | bytes 3145728 | tf_op jit(solution)/shard_map/dot_general | solution.py:38
  58.6 1.0 %convolution_add_fusion.1 = f32[512,512]{1,0:T(8,128)S(1)} fusion(f32[512,512]{1,0:T(8,128)S(1)} %convolution_add_fusion.2, f32[512,512]{1,0:T(8,128)S(1)} %fusion.1), kind=kOutput, calls=%fused_computation.4 | convolution fusion | flops 805830656 | bytes 3145728 | tf_op jit(solution)/shard_map/dot_general | solution.py:38
  59.7 0.0 copy-start.2
  59.7 1.0 %convolution_add_fusion.3 = f32[512,512]{1,0:T(8,128)S(1)} fusion(f32[512,512]{1,0:T(8,128)S(1)} %fusion.1, f32[512,512]{1,0:T(8,128)S(1)} %fusion.2), kind=kOutput, calls=%fused_computation.6 | convolution fusion | flops 807403520 | bytes 3145728 | tf_op jit(solution)/shard_map/dot_general | solution.py:38
  60.7 1.1 %fusion = f32[512,512]{1,0:T(8,128)S(1)} fusion(f32[512,512]{1,0:T(8,128)S(1)} %convolution_add_fusion.1), kind=kOutput, calls=%fused_computation.3 | convolution fusion | flops 806092800 | bytes 2097152 | tf_op jit(solution)/shard_map/dot_general | solution.py:38
  61.8 1.0 %fusion.3 = bf16[512,512]{1,0:T(8,128)(2,1)S(1)} fusion(f32[512,512]{1,0:T(8,128)S(1)} %fusion, f32[512,512]{1,0:T(8,128)S(1)} %convolution_add_fusion.3), kind=kOutput, calls=%fused_computation.13 | convolution fusion | flops 806092800 | bytes 2621440 | tf_op jit(solution)/shard_map/dot_general | solution.py:38
  62.9 0.0 copy-done.2
  62.9 3.8 %subtract_multiply_fusion = f32[512,2048]{1,0:T(8,128)} fusion(f32[512,2048]{1,0:T(8,128)S(1)} %copy-done.2, bf16[512,512]{1,0:T(8,128)(2,1)S(1)} %fusion.3, bf16[512,2048]{1,0:T(8,128)(2,1)S(1)} %get-tuple-element.21, f32[2048]{0:T(1024)S(1)} %dynamic_slice.3, f32[]{:T(128)} %bitcast.1), kind=kOutput, calls=%fused_computation | convolution fusion | flops 1081081856 | bytes 11018244 | tf_op jit(solution)/shard_map/dot_general | solution.py:335
  66.7 0.8 %copy.11 = f32[64,2048]{1,0:T(8,128)} copy(f32[64,2048]{1,0:T(8,128)S(1)} %get-tuple-element.27) | data formatting | bytes 1048576
  (5 shorter events, 0.1 us)
Async XLA Ops:
  1.9 1.6 %copy-start = (bf16[1,512,2048]{2,1,0:T(8,128)(2,1)S(1)}, bf16[1,512,2048]{2,1,0:T(8,128)(2,1)}, u32[]{:S(2)}) copy-start(bf16[1,512,2048]{2,1,0:T(8,128)(2,1)} %param.7) | copy-start | bytes 6291460
  3.5 1.0 %copy-start.1 = (f32[64,2048]{1,0:T(8,128)S(1)}, f32[64,2048]{1,0:T(8,128)}, u32[]{:S(2)}) copy-start(f32[64,2048]{1,0:T(8,128)} %momentum.1) | copy-start | bytes 1572868
  59.7 3.2 %copy-start.2 = (f32[512,2048]{1,0:T(8,128)S(1)}, f32[512,2048]{1,0:T(8,128)}, u32[]{:S(2)}) copy-start(f32[512,2048]{1,0:T(8,128)} %param.9) | copy-start | bytes 12582916

commit v2 on v1

--- a/solution.py
+++ b/solution.py
@@ -38,30 +38,39 @@
     return jnp.dot(left, right, precision=lax.Precision.HIGH, preferred_element_type=jnp.float32)
 
 
-def polynomial_of_gram(gram):
+def short_product(left, right):
+    return jnp.dot(
+        left.astype(jnp.bfloat16), right.astype(jnp.bfloat16), preferred_element_type=jnp.float32
+    )
+
+
+def polynomial_of_gram(gram_total, scale):
     lead, second, third = quintic_terms
     whole = None
+    gram = gram_total.astype(jnp.float32) * scale
+    square = scale * scale * jnp.dot(gram_total, gram_total, preferred_element_type=jnp.float32)
     for iteration in range(ITERS):
-        rest = second * gram + third * product(gram, gram)
+        multiply = product if iteration == ITERS - 1 else short_product
+        rest = second * gram + third * (square if iteration == 0 else multiply(gram, gram))
         if whole is None:
             whole = lead * jnp.eye(KVL, dtype=jnp.float32) + rest
         else:
-            whole = lead * whole + product(rest, whole)
+            whole = lead * whole + multiply(rest, whole)
         if iteration < ITERS - 1:
-            half = lead * gram + product(rest, gram)
-            gram = lead * half + product(half, rest)
+            half = lead * gram + multiply(rest, gram)
+            gram = lead * half + multiply(half, rest)
     return whole
 
 
-CHUNKS = 2
+CHUNKS = 4
 MESH = pl.DeviceIdType.MESH
 
 
 def exchange(
     dp_count,
     fsdp_count,
-    grad,
-    momentum,
+    grad_all,
+    momentum_all,
     peaks,
     new_momentum,
     columns,
@@ -76,6 +85,10 @@
     stats_in,
     stats_wide,
     stats_wide_in,
+    kept,
+    momentum,
+    kept_sem,
+    momentum_sem,
     pair_send,
     pair_recv,
     rs_send,
@@ -104,6 +117,15 @@
     width = momentum.shape[1] // CHUNKS
     partner = 2 * q + 1 - core
 
+    kept_copies = []
+    for k in range(chips):
+        device = 2 * lax.rem(q + k, chips) + core
+        source = grad_all.at[0, pl.ds(pl.multiple_of(device * rows, rows), rows)]
+        kept_copies.append(pltpu.make_async_copy(source, kept.at[k], kept_sem.at[k]))
+    momentum_copy = pltpu.make_async_copy(momentum_all, momentum, momentum_sem)
+    for copy in kept_copies + [momentum_copy]:
+        copy.start()
+
     barrier = pltpu.get_barrier_semaphore()
     for k in range(1, dp_count):
         pl.semaphore_signal(
@@ -144,17 +166,19 @@
     for h in range(CHUNKS):
         for k in offsets:
             paired[h, k] = send(
-                grad.at[block(2 * ahead(k) + 1 - core), chunk(h)],
+                grad_all.at[0, block(2 * ahead(k) + 1 - core), chunk(h)],
                 pair.at[h, k],
                 pair_send.at[h, k],
                 pair_recv.at[h, k],
                 (partner, f),
             )
     scattered = {}
+    for copy in kept_copies:
+        copy.wait()
     for h in range(CHUNKS):
         for k in range(1, chips):
             paired[h, k].wait_recv()
-            here = grad[block(2 * ahead(k) + core), chunk(h)].astype(jnp.float32)
+            here = kept[k, :, chunk(h)].astype(jnp.float32)
             outgoing[h, k] = (here + pair[h, k].astype(jnp.float32)).astype(jnp.bfloat16)
             scattered[h, k] = send(
                 outgoing.at[h, k],
@@ -166,9 +190,19 @@
     gathered = {}
     forwarded = {}
     square_sum = jnp.float32(0.0)
+    momentum_copy.wait()
+
+    def forward(h):
+        for k in range(1, chips):
+            gathered[h, k].wait_recv()
+            there = columns.at[block(2 * behind(k) + core), chunk(h)]
+            forwarded[h, k] = send(
+                there, there, fw_send.at[h, k], fw_recv.at[h, k], (partner, f)
+            )
+
     for h in range(CHUNKS):
         paired[h, 0].wait_recv()
-        summed = grad[block(d), chunk(h)].astype(jnp.float32) + pair[h, 0].astype(jnp.float32)
+        summed = kept[0, :, chunk(h)].astype(jnp.float32) + pair[h, 0].astype(jnp.float32)
         for k in range(1, chips):
             scattered[h, k].wait_recv()
             summed = summed + incoming[h, k].astype(jnp.float32)
@@ -183,8 +217,11 @@
             )
         forwarded[h, 0] = send(mine, mine, fw_send.at[h, 0], fw_recv.at[h, 0], (partner, f))
         square_sum = square_sum + jnp.sum(blended * blended)
-
-    stats[0:8] = peaks[...]
+        if h >= 2:
+            forward(h - 2)
+
+    stats[0:8] = jnp.zeros((8, 128), jnp.float32)
+    stats[0:1, 0:HEADS] = peaks[...].astype(jnp.float32)
     stats[8:16] = jnp.full((8, 128), square_sum, jnp.float32)
     stat_copies = [
         send(
@@ -198,13 +235,8 @@
     ]
 
     own_gram = jnp.zeros((rows, gram.shape[0]), jnp.float32)
-    for h in range(CHUNKS):
-        for k in range(1, chips):
-            gathered[h, k].wait_recv()
-            there = columns.at[block(2 * behind(k) + core), chunk(h)]
-            forwarded[h, k] = send(
-                there, there, fw_send.at[h, k], fw_recv.at[h, k], (partner, f)
-            )
+    for h in range(max(CHUNKS - 2, 0), CHUNKS):
+        forward(h)
     for copy in stat_copies:
         copy.wait_recv()
     top = stats[0:8]
@@ -299,7 +331,7 @@
             jax.ShapeDtypeStruct((KVL, KVL), jnp.bfloat16),
             jax.ShapeDtypeStruct((16, 128), jnp.float32),
         ),
-        in_specs=[in_vmem] * 3,
+        in_specs=[pl.BlockSpec(memory_space=pl.ANY)] * 2 + [in_vmem],
         out_specs=(in_vmem,) * 4,
         scratch_shapes=[
             slots,
@@ -311,6 +343,10 @@
             pltpu.VMEM((dp_count, 16, 128), jnp.float32),
             pltpu.VMEM((16, 128), jnp.float32),
             pltpu.VMEM((fsdp_count, 16, 128), jnp.float32),
+            pltpu.VMEM((chips, rows, shard_cols), jnp.bfloat16),
+            pltpu.VMEM((rows, shard_cols), jnp.float32),
+            pltpu.SemaphoreType.DMA((chips,)),
+            pltpu.SemaphoreType.DMA,
         ]
         + by_chunk
         + by_fsdp
@@ -318,20 +354,18 @@
         + by_fsdp
         + by_chip,
         compiler_params=pltpu.CompilerParams(
-            collective_id=0, has_side_effects=True, vmem_limit_bytes=40 * 1024 * 1024
+            collective_id=0, has_side_effects=True, vmem_limit_bytes=24 * 1024 * 1024
         ),
     )(gradient, momentum, peaks)
 
 
 def local(gradients, momentum, weight, logit_peaks, clip_threshold):
-    peaks = jnp.zeros((8, 128), jnp.float32).at[:1, :HEADS].set(logit_peaks.astype(jnp.float32))
-    new_momentum, columns, gram_total, stats = reduce_and_gather(gradients[0], momentum, peaks)
+    new_momentum, columns, gram_total, stats = reduce_and_gather(gradients, momentum, logit_peaks)
     largest = stats[0, :HEADS]
     square_total = stats[8, 0]
     update_norm = jnp.sqrt(square_total / (KVL * KVO)).reshape(1)
     inverse = 1.0 / (jnp.sqrt(square_total) + epsilon)
-    gram = gram_total.astype(jnp.float32) * inverse * inverse
-    whole = polynomial_of_gram(gram)
+    whole = polynomial_of_gram(gram_total, inverse * inverse)
     orthogonal = inverse * jnp.dot(
         whole.astype(jnp.bfloat16), columns, preferred_element_type=jnp.float32
     )

time: 68.9 us -> 64.9 us (0.942)
  matrix products: 13.3 us -> 9.07 us
    dot_general x9 -> x2, matrix products: 9.45 us -> 2.15 us  [product(): jnp.dot(left, right, precision=lax.Precision.HIGH, preferred_element_type...]
    dot_general x0 -> x7, matrix products: none -> 3.14 us  [the longest x6 2.66 us: short_product(): jnp.dot(left.astype(jnp.bfloat16), right.astype(jnp.bfloat16), preferred_...]
    unnamed x9 -> x11, local copies, waits for them, and re-layouts: 3.46 us -> 4.11 us
where the time goes in v2:
time: 64.9 us; the launch traced here: 64.6 us
  Pallas kernels  46.9 us (72%)
  matrix products  9.07 us (14%)
  local copies, waits for them, and re-layouts  4.71 us (7%)
  between operations  3.96 us (6%)
    pallas_call x1, Pallas kernels, reduce_and_gather(): pl.pallas_call(functools.partial(exchange, dp_count, fsdp_count), out_sha...  46.9 us
    unnamed x11, local copies, waits for them, and re-layouts  4.11 us
    dot_general x1, matrix products, local(): jnp.dot(whole.astype(jnp.bfloat16), columns, preferred_element_type=jnp.f...  3.78 us
    dot_general x6, matrix products, short_product(): jnp.dot(left.astype(jnp.bfloat16), right.astype(jnp.bfloat16), preferred_...  2.66 us
    dot_general x2, matrix products, product(): jnp.dot(left, right, precision=lax.Precision.HIGH, preferred_element_type...  2.15 us

profile of v2, /device:TPU:0, one launch (start us, length us, event | category | flops | bytes accessed | tf_op | source)
XLA Modules:
  0.0 64.6 jit_solution(13522603155238787386)
XLA Ops:
  1.3 0.0 copy-start
  1.3 1.6 %copy-done = bf16[1,512,2048]{2,1,0:T(8,128)(2,1)S(1)} copy-done((bf16[1,512,2048]{2,1,0:T(8,128)(2,1)S(1)}, bf16[1,512,2048]{2,1,0:T(8,128)(2,1)}, u32[]{:S(2)}) %copy-start) | copy-done | bytes 2097176
  2.9 0.0 copy-start.1
  2.9 1.0 %copy-done.1 = f32[64,2048]{1,0:T(8,128)S(1)} copy-done((f32[64,2048]{1,0:T(8,128)S(1)}, f32[64,2048]{1,0:T(8,128)}, u32[]{:S(2)}) %copy-start.1) | copy-done | bytes 524312
  3.9 0.0 copy-start.2
  3.9 0.7 %copy-done.2 = s32[1,32]{1,0:T(1,128)S(1)} copy-done((s32[1,32]{1,0:T(1,128)S(1)}, s32[1,32]{1,0:T(1,128)}, u32[]{:S(2)}) %copy-start.2) | copy-done | bytes 152
  4.6 46.9 %shard_map.76 = (f32[64,2048]{1,0:T(8,128)S(1)}, bf16[512,2048]{1,0:T(8,128)(2,1)S(1)}, bf16[512,512]{1,0:T(8,128)(2,1)S(1)}, f32[16,128]{1,0:T(8,128)S(1)}) custom-call(bf16[1,512,2048]{2,1,0:T(8,128)(2,1)S(1)} %copy-done, f32[64,2048]{1,0:T(8,128)S(1)} %copy-done.1, s32[1,32]{1,0:T(1,128)S(1)} %copy-done.2), custom_call_target="tpu_custom_call" | custom-call | tf_op jit(solution)/shard_map/pallas_call | solution.py:326
  51.4 0.5 slice.6
  53.4 0.1 broadcast_in_dim.2
  53.5 0.5 fusion.3
  54.0 0.5 convolution_add_fusion.5
  54.5 0.4 convolution_add_fusion.4
  54.9 0.4 fusion.4
  55.4 0.4 convolution_add_fusion.2
  55.8 0.4 convolution_add_fusion.1
  56.3 0.0 copy-start.3
  56.3 0.4 convolution_add_fusion.3
  56.7 1.1 %fusion = f32[512,512]{1,0:T(8,128)S(1)} fusion(f32[512,512]{1,0:T(8,128)S(1)} %convolution_add_fusion.1), kind=kOutput, calls=%fused_computation.3 | convolution fusion | flops 806092800 | bytes 2097152 | tf_op jit(solution)/shard_map/dot_general | solution.py:38
  57.9 1.0 %fusion.5 = bf16[512,512]{1,0:T(8,128)(2,1)S(1)} fusion(f32[512,512]{1,0:T(8,128)S(1)} %fusion, f32[512,512]{1,0:T(8,128)S(1)} %convolution_add_fusion.3), kind=kOutput, calls=%fused_computation.15 | convolution fusion | flops 806092800 | bytes 2621440 | tf_op jit(solution)/shard_map/dot_general | solution.py:38
  58.9 0.0 copy-done.3
  58.9 3.8 %subtract_multiply_fusion = f32[512,2048]{1,0:T(8,128)} fusion(f32[512,2048]{1,0:T(8,128)S(1)} %copy-done.3, bf16[512,512]{1,0:T(8,128)(2,1)S(1)} %fusion.5, bf16[512,2048]{1,0:T(8,128)(2,1)S(1)} %get-tuple-element.9, f32[2048]{0:T(1024)S(1)} %dynamic_slice.3, f32[]{:T(128)} %bitcast), kind=kOutput, calls=%fused_computation | convolution fusion | flops 1081081856 | bytes 11018244 | tf_op jit(solution)/shard_map/dot_general | solution.py:369
  62.7 0.8 %copy.11 = f32[64,2048]{1,0:T(8,128)} copy(f32[64,2048]{1,0:T(8,128)S(1)} %get-tuple-element.15) | data formatting | bytes 1048576
  (4 shorter events, 0.1 us)
Async XLA Ops:
  1.3 1.6 %copy-start = (bf16[1,512,2048]{2,1,0:T(8,128)(2,1)S(1)}, bf16[1,512,2048]{2,1,0:T(8,128)(2,1)}, u32[]{:S(2)}) copy-start(bf16[1,512,2048]{2,1,0:T(8,128)(2,1)} %grad_all.1) | copy-start | bytes 6291460
  2.9 1.0 %copy-start.1 = (f32[64,2048]{1,0:T(8,128)S(1)}, f32[64,2048]{1,0:T(8,128)}, u32[]{:S(2)}) copy-start(f32[64,2048]{1,0:T(8,128)} %momentum_all.1) | copy-start | bytes 1572868
  3.9 0.7 %copy-start.2 = (s32[1,32]{1,0:T(1,128)S(1)}, s32[1,32]{1,0:T(1,128)}, u32[]{:S(2)}) copy-start(s32[1,32]{1,0:T(1,128)} %peaks.1) | copy-start | bytes 388
  56.3 2.6 %copy-start.3 = (f32[512,2048]{1,0:T(8,128)S(1)}, f32[512,2048]{1,0:T(8,128)}, u32[]{:S(2)}) copy-start(f32[512,2048]{1,0:T(8,128)} %param.7) | copy-start | bytes 12582916

commit v3 on v2

--- a/solution.py
+++ b/solution.py
@@ -117,15 +117,6 @@
     width = momentum.shape[1] // CHUNKS
     partner = 2 * q + 1 - core
 
-    kept_copies = []
-    for k in range(chips):
-        device = 2 * lax.rem(q + k, chips) + core
-        source = grad_all.at[0, pl.ds(pl.multiple_of(device * rows, rows), rows)]
-        kept_copies.append(pltpu.make_async_copy(source, kept.at[k], kept_sem.at[k]))
-    momentum_copy = pltpu.make_async_copy(momentum_all, momentum, momentum_sem)
-    for copy in kept_copies + [momentum_copy]:
-        copy.start()
-
     barrier = pltpu.get_barrier_semaphore()
     for k in range(1, dp_count):
         pl.semaphore_signal(
@@ -155,11 +146,25 @@
     def chunk(h):
         return pl.ds(h * width, width)
 
+    square_plane = chips == 4
+
     def ahead(k):
+        if square_plane:
+            return (q, q + 1 - 2 * (q % 2), q + 2 - 4 * (q // 2), 3 - q)[k]
         return lax.rem(q + k, chips)
 
     def behind(k):
+        if square_plane:
+            return ahead(k)
         return lax.rem(q + chips - k, chips)
+
+    kept_copies = []
+    for k in range(chips):
+        source = grad_all.at[0, block(2 * ahead(k) + core)]
+        kept_copies.append(pltpu.make_async_copy(source, kept.at[k], kept_sem.at[k]))
+    momentum_copy = pltpu.make_async_copy(momentum_all, momentum, momentum_sem)
+    for copy in kept_copies + [momentum_copy]:
+        copy.start()
 
     offsets = list(range(1, chips)) + [0]
     paired = {}
@@ -192,14 +197,20 @@
     square_sum = jnp.float32(0.0)
     momentum_copy.wait()
 
-    def forward(h):
-        for k in range(1, chips):
+    def forward(h, which):
+        for k in which:
             gathered[h, k].wait_recv()
             there = columns.at[block(2 * behind(k) + core), chunk(h)]
+            if square_plane and k == 1 + h % 2:
+                gathered[h, 3] = send(
+                    there, there, ag_send.at[h, 3], ag_recv.at[h, 3], (2 * ahead(3 - k) + core, f)
+                )
             forwarded[h, k] = send(
                 there, there, fw_send.at[h, k], fw_recv.at[h, k], (partner, f)
             )
 
+    direct = range(1, 3 if square_plane else chips)
+    relayed = range(3, chips) if square_plane else ()
     for h in range(CHUNKS):
         paired[h, 0].wait_recv()
         summed = kept[0, :, chunk(h)].astype(jnp.float32) + pair[h, 0].astype(jnp.float32)
@@ -211,14 +222,14 @@
         blended = summed + momentum_decay * updated
         columns[block(d), chunk(h)] = blended.astype(jnp.bfloat16)
         mine = columns.at[block(d), chunk(h)]
-        for k in range(1, chips):
+        for k in direct:
             gathered[h, k] = send(
                 mine, mine, ag_send.at[h, k], ag_recv.at[h, k], (2 * ahead(k) + core, f)
             )
         forwarded[h, 0] = send(mine, mine, fw_send.at[h, 0], fw_recv.at[h, 0], (partner, f))
         square_sum = square_sum + jnp.sum(blended * blended)
         if h >= 2:
-            forward(h - 2)
+            forward(h - 2, direct)
 
     stats[0:8] = jnp.zeros((8, 128), jnp.float32)
     stats[0:1, 0:HEADS] = peaks[...].astype(jnp.float32)
@@ -236,7 +247,9 @@
 
     own_gram = jnp.zeros((rows, gram.shape[0]), jnp.float32)
     for h in range(max(CHUNKS - 2, 0), CHUNKS):
-        forward(h)
+        forward(h, direct)
+    for h in range(CHUNKS):
+        forward(h, relayed)
     for copy in stat_copies:
         copy.wait_recv()
     top = stats[0:8]

time: 64.9 us -> 64.4 us (level)
  no operation moved by 1% of the time
where the time goes in v3:
time: 64.4 us; the launch traced here: 64.1 us
  Pallas kernels  46.4 us (72%)
  matrix products  9.07 us (14%)
  local copies, waits for them, and re-layouts  4.71 us (7%)
  between operations  3.96 us (6%)
    pallas_call x1, Pallas kernels, reduce_and_gather(): pl.pallas_call(functools.partial(exchange, dp_count, fsdp_count), out_sha...  46.4 us
    unnamed x11, local copies, waits for them, and re-layouts  4.11 us
    dot_general x1, matrix products, local(): jnp.dot(whole.astype(jnp.bfloat16), columns, preferred_element_type=jnp.f...  3.78 us
    dot_general x6, matrix products, short_product(): jnp.dot(left.astype(jnp.bfloat16), right.astype(jnp.bfloat16), preferred_...  2.66 us
    dot_general x2, matrix products, product(): jnp.dot(left, right, precision=lax.Precision.HIGH, preferred_element_type...  2.15 us

profile of v3, /device:TPU:0, one launch (start us, length us, event | category | flops | bytes accessed | tf_op | source)
XLA Modules:
  0.0 64.1 jit_solution(15661076638019765458)
XLA Ops:
  1.3 0.0 copy-start
  1.3 1.6 %copy-done = bf16[1,512,2048]{2,1,0:T(8,128)(2,1)S(1)} copy-done((bf16[1,512,2048]{2,1,0:T(8,128)(2,1)S(1)}, bf16[1,512,2048]{2,1,0:T(8,128)(2,1)}, u32[]{:S(2)}) %copy-start) | copy-done | bytes 2097176
  2.9 0.0 copy-start.1
  2.9 1.0 %copy-done.1 = f32[64,2048]{1,0:T(8,128)S(1)} copy-done((f32[64,2048]{1,0:T(8,128)S(1)}, f32[64,2048]{1,0:T(8,128)}, u32[]{:S(2)}) %copy-start.1) | copy-done | bytes 524312
  3.9 0.0 copy-start.2
  3.9 0.7 %copy-done.2 = s32[1,32]{1,0:T(1,128)S(1)} copy-done((s32[1,32]{1,0:T(1,128)S(1)}, s32[1,32]{1,0:T(1,128)}, u32[]{:S(2)}) %copy-start.2) | copy-done | bytes 152
  4.6 46.4 %shard_map.76 = (f32[64,2048]{1,0:T(8,128)S(1)}, bf16[512,2048]{1,0:T(8,128)(2,1)S(1)}, bf16[512,512]{1,0:T(8,128)(2,1)S(1)}, f32[16,128]{1,0:T(8,128)S(1)}) custom-call(bf16[1,512,2048]{2,1,0:T(8,128)(2,1)S(1)} %copy-done, f32[64,2048]{1,0:T(8,128)S(1)} %copy-done.1, s32[1,32]{1,0:T(1,128)S(1)} %copy-done.2), custom_call_target="tpu_custom_call" | custom-call | tf_op jit(solution)/shard_map/pallas_call | solution.py:339
  51.0 0.5 slice.6
  52.9 0.1 broadcast_in_dim.2
  53.0 0.5 fusion.3
  53.5 0.5 convolution_add_fusion.5
  54.0 0.4 convolution_add_fusion.4
  54.4 0.4 fusion.4
  54.9 0.4 convolution_add_fusion.2
  55.4 0.4 convolution_add_fusion.1
  55.8 0.0 copy-start.3
  55.8 0.4 convolution_add_fusion.3
  56.3 1.1 %fusion = f32[512,512]{1,0:T(8,128)S(1)} fusion(f32[512,512]{1,0:T(8,128)S(1)} %convolution_add_fusion.1), kind=kOutput, calls=%fused_computation.3 | convolution fusion | flops 806092800 | bytes 2097152 | tf_op jit(solution)/shard_map/dot_general | solution.py:38
  57.4 1.0 %fusion.5 = bf16[512,512]{1,0:T(8,128)(2,1)S(1)} fusion(f32[512,512]{1,0:T(8,128)S(1)} %fusion, f32[512,512]{1,0:T(8,128)S(1)} %convolution_add_fusion.3), kind=kOutput, calls=%fused_computation.15 | convolution fusion | flops 806092800 | bytes 2621440 | tf_op jit(solution)/shard_map/dot_general | solution.py:38
  58.4 0.0 copy-done.3
  58.4 3.8 %subtract_multiply_fusion = f32[512,2048]{1,0:T(8,128)} fusion(f32[512,2048]{1,0:T(8,128)S(1)} %copy-done.3, bf16[512,512]{1,0:T(8,128)(2,1)S(1)} %fusion.5, bf16[512,2048]{1,0:T(8,128)(2,1)S(1)} %get-tuple-element.9, f32[2048]{0:T(1024)S(1)} %dynamic_slice.3, f32[]{:T(128)} %bitcast), kind=kOutput, calls=%fused_computation | convolution fusion | flops 1081081856 | bytes 11018244 | tf_op jit(solution)/shard_map/dot_general | solution.py:382
  62.2 0.8 %copy.11 = f32[64,2048]{1,0:T(8,128)} copy(f32[64,2048]{1,0:T(8,128)S(1)} %get-tuple-element.15) | data formatting | bytes 1048576
  (4 shorter events, 0.1 us)
Async XLA Ops:
  1.3 1.6 %copy-start = (bf16[1,512,2048]{2,1,0:T(8,128)(2,1)S(1)}, bf16[1,512,2048]{2,1,0:T(8,128)(2,1)}, u32[]{:S(2)}) copy-start(bf16[1,512,2048]{2,1,0:T(8,128)(2,1)} %grad_all.1) | copy-start | bytes 6291460
  2.9 1.0 %copy-start.1 = (f32[64,2048]{1,0:T(8,128)S(1)}, f32[64,2048]{1,0:T(8,128)}, u32[]{:S(2)}) copy-start(f32[64,2048]{1,0:T(8,128)} %momentum_all.1) | copy-start | bytes 1572868
  3.9 0.7 %copy-start.2 = (s32[1,32]{1,0:T(1,128)S(1)}, s32[1,32]{1,0:T(1,128)}, u32[]{:S(2)}) copy-start(s32[1,32]{1,0:T(1,128)} %peaks.1) | copy-start | bytes 388
  55.8 2.6 %copy-start.3 = (f32[512,2048]{1,0:T(8,128)S(1)}, f32[512,2048]{1,0:T(8,128)}, u32[]{:S(2)}) copy-start(f32[512,2048]{1,0:T(8,128)} %param.7) | copy-start | bytes 12582916
